TPU v7x, 32 devices: a whole 2x2x4 slice. The times are simulated.
32 devices in a mesh: grp: 8 (over y, x, core), seq: 4 (over z).
Axes of the slice: x: 2, y: 2, z: 4, core: 2. Of those that a mesh axis runs over, the one named last changes fastest.
Arguments:
- tokens: bfloat16 [8192, 2048], P(('grp', 'seq')), may hold values from -6 to 6
- cotangent: bfloat16 [8192, 2048], P(('grp', 'seq')), may hold values from -6 to 6
- segment_ids: int32 [8192], P(('grp', 'seq')), may hold values from 0 to 31, never falling along the last dimension, each value on 1 to 768 neighbouring positions
- tile_owner_slots: int32 [166], replicated, may hold values from 0 to 167, as said below
- weights_low: bfloat16 [168, 2048, 128], P('grp', 'seq')
- master: float32 [168, 2048, 128], P('grp', 'seq')
- moment_one: float32 [168, 2048, 128], P('grp', 'seq')
- moment_two: float32 [168, 2048, 128], P('grp', 'seq'), as said below
- left_basis_set: float32 [168, 2048, 512], P('grp', 'seq'), as said below
- right_basis_set: float32 [168, 512, 128], P('grp', 'seq'), as said below
- gains: float32 [2, 2048], replicated, may hold values from 0.5 to 1.5
- gain_moment_one: float32 [2, 2048], replicated, may hold values from -28 to 28
- gain_moment_two: float32 [2, 2048], replicated, may hold values from 430.8992 to 1720.32
Outputs:
- block_out: bfloat16 [8192, 2048], P(('grp', 'seq'))
- input_grad: float32 [8192, 2048], P(('grp', 'seq'))
- new_master: float32 [168, 2048, 128], P('grp', 'seq')
- new_moment_one: float32 [168, 2048, 128], P('grp', 'seq')
- new_moment_two: float32 [168, 2048, 128], P('grp', 'seq')
- gain_grads: float32 [2, 2048], replicated
- new_gains: float32 [2, 2048], replicated
- new_gain_one: float32 [2, 2048], replicated
- new_gain_two: float32 [2, 2048], replicated
Inputs may be any that keep to these rules, and one draw needn't show every extreme that they name: `tile_owner_slots`: the entries are distinct; slot q belongs to data group q // 21. `segment_ids`: never falls along the tokens. `left_basis_set`: each 512 x 512 block is orthogonal. `right_basis_set`: each 128 x 128 block is orthogonal. `moment_two`: positive.
All inputs are finite; a program needn't handle non-finite values.
Results may differ from a plain program's by a relative error of at most 0.015.
Values may be sent and summed in bfloat16 or wider, within the bound.
A program may use at most 704 MiB of HBM per device.

v0:
```python
import jax
import jax.numpy as jnp
from jax import lax
from jax.sharding import PartitionSpec as P

MODEL_WIDTH = 2048
NH = 16
HD = 128
FF = 5632
SEQLEN = 1024
NORM_EPS = 1e-05
BETA_ONE = 0.95
BETA_TWO = 0.95
ADAM_EPS = 1e-08
WEIGHT_DECAY = 0.01
LEARN_RATE = 0.03
GAIN_RATE = 1.5
ROPE_BASE = 10000.0
MASKED = -1e30
PRECISE = lax.Precision.HIGHEST


def rotate(values, positions, direction):
    head_width = values.shape[-1]
    half_width = head_width // 2
    frequency = ROPE_BASE ** (-(jnp.arange(half_width, dtype=jnp.float32) * 2.0) / head_width)
    angles = positions.astype(jnp.float32)[:, None] * frequency[None, :]
    cosine = jnp.cos(angles)[:, None, :]
    sine_part = (jnp.sin(angles) * direction)[:, None, :]
    leading = values[..., :half_width]
    trailing = values[..., half_width:]
    return jnp.concatenate(
        [leading * cosine - trailing * sine_part, trailing * cosine + leading * sine_part], axis=-1
    )


def visible(query_index, key_index, query_seg, key_seg):
    causal = query_index[:, None] >= key_index[None, :]
    same_seq = query_index[:, None] // SEQLEN == key_index[None, :] // SEQLEN
    same_doc = query_seg[:, None] == key_seg[None, :]
    return causal & same_seq & same_doc


def contract(left_side, right_side):
    return lax.dot_general(
        left_side, right_side, (((0,), (0,)), ((), ())), preferred_element_type=jnp.float32
    )


def times_transpose(left_side, right_side):
    return lax.dot_general(
        left_side, right_side, (((1,), (1,)), ((), ())), preferred_element_type=jnp.float32
    )


def attend(queries, key_rows, value_rows, query_index, query_seg, key_index, key_seg):
    query_total, head_count, head_width = queries.shape
    block_rows = min(512, query_total)
    block_count = query_total // block_rows
    score_scale = head_width ** (-0.5)

    def one_block(inputs):
        block_queries, block_index, block_seg = inputs
        raw_scores = jnp.einsum(
            "qhd,kd->hqk", block_queries, key_rows, preferred_element_type=jnp.float32
        )
        allowed = visible(block_index, key_index, block_seg, key_seg)
        score_matrix = jnp.where(allowed[None], raw_scores * score_scale, MASKED)
        highest = jnp.max(score_matrix, axis=-1, keepdims=True)
        exponent = jnp.exp(score_matrix - highest)
        totals = jnp.sum(exponent, axis=-1, keepdims=True)
        probs_low = (exponent / totals).astype(jnp.bfloat16)
        context = jnp.einsum(
            "hqk,kd->qhd", probs_low, value_rows, preferred_element_type=jnp.float32
        )
        return (context, jnp.transpose((highest + jnp.log(totals))[..., 0]))

    context, log_totals = lax.map(
        one_block,
        (
            queries.reshape(block_count, block_rows, head_count, head_width),
            query_index.reshape(block_count, block_rows),
            query_seg.reshape(block_count, block_rows),
        ),
    )
    return (
        context.reshape(query_total, head_count, head_width),
        log_totals.reshape(query_total, head_count),
    )


def attend_back(
    queries, key_rows, value_rows, grads_low, log_totals, query_index, query_seg, key_index, key_seg
):
    query_total, head_count, head_width = queries.shape
    block_rows = min(512, query_total)
    block_count = query_total // block_rows
    score_scale = head_width ** (-0.5)

    def one_block(running, inputs):
        block_queries, block_grads, block_totals, block_index, block_seg = inputs
        raw_scores = jnp.einsum(
            "qhd,kd->hqk", block_queries, key_rows, preferred_element_type=jnp.float32
        )
        allowed = visible(block_index, key_index, block_seg, key_seg)
        shifted = raw_scores * score_scale - jnp.transpose(block_totals)[:, :, None]
        probs = jnp.where(allowed[None], jnp.exp(shifted), 0.0)
        prob_grad = jnp.einsum(
            "qhd,kd->hqk", block_grads, value_rows, preferred_element_type=jnp.float32
        )
        centre = jnp.sum(probs * prob_grad, axis=-1, keepdims=True)
        score_grad = (probs * (prob_grad - centre) * score_scale).astype(jnp.bfloat16)
        query_part = jnp.einsum(
            "hqk,kd->qhd", score_grad, key_rows, preferred_element_type=jnp.float32
        )
        key_part = running[0] + jnp.einsum(
            "hqk,qhd->kd", score_grad, block_queries, preferred_element_type=jnp.float32
        )
        value_part = running[1] + jnp.einsum(
            "hqk,qhd->kd",
            probs.astype(jnp.bfloat16),
            block_grads,
            preferred_element_type=jnp.float32,
        )
        return ((key_part, value_part), query_part)

    zeros_rows = jnp.zeros(key_rows.shape, jnp.float32)
    (key_grad, value_grad), query_grad = lax.scan(
        one_block,
        (zeros_rows, zeros_rows),
        (
            queries.reshape(block_count, block_rows, head_count, head_width),
            grads_low.reshape(block_count, block_rows, head_count, head_width),
            log_totals.reshape(block_count, block_rows, head_count),
            query_index.reshape(block_count, block_rows),
            query_seg.reshape(block_count, block_rows),
        ),
    )
    return (query_grad.reshape(query_total, head_count, head_width), key_grad, value_grad)


def local(
    tokens,
    cotangent,
    segment_ids,
    tile_owner_slots,
    weights_low,
    master,
    moment_one,
    moment_two,
    left_basis_set,
    right_basis_set,
    gains,
    gain_moment_one,
    gain_moment_two,
):
    grp_count = lax.axis_size("grp")
    seq_count = lax.axis_size("seq")
    grp_here = lax.axis_index("grp")
    rows_here = tokens.shape[0]
    slots_here, rows_block, tile_width = weights_low.shape
    query_cols = NH * HD
    value_end = query_cols + 2 * HD
    output_end = value_end + MODEL_WIDTH
    attn_tiles = output_end // tile_width
    hidden_tiles = FF // tile_width
    share = -(-hidden_tiles // grp_count)
    share_cols = share * tile_width
    sub_rows = rows_block // grp_count
    local_index = lax.axis_index("seq") * rows_here + jnp.arange(rows_here, dtype=jnp.int32)
    local_place = local_index % SEQLEN
    plane_tiles = lax.all_gather(weights_low, "grp", axis=0, tiled=True)
    hidden_ids = grp_here * share + jnp.arange(share, dtype=jnp.int32)
    real = hidden_ids < hidden_tiles
    hidden_ids = jnp.minimum(hidden_ids, hidden_tiles - 1)
    feed_ids = (
        attn_tiles + jnp.arange(3, dtype=jnp.int32)[:, None] * hidden_tiles + hidden_ids[None, :]
    ).reshape(-1)
    attn_rows = lax.dynamic_slice_in_dim(plane_tiles, grp_here * sub_rows, sub_rows, axis=1)
    attn_rows = jnp.transpose(attn_rows[tile_owner_slots[:attn_tiles]], (1, 0, 2)).reshape(
        sub_rows, output_end
    )
    attn_weights = lax.all_gather(attn_rows, "seq", axis=0, tiled=False)
    attn_weights = lax.all_gather(attn_weights, "grp", axis=1, tiled=True).reshape(
        MODEL_WIDTH, output_end
    )
    feed_tiles = jnp.where(
        jnp.tile(real, 3)[:, None, None], plane_tiles[tile_owner_slots[feed_ids]], 0
    )
    feed_rows = jnp.transpose(feed_tiles, (1, 0, 2)).reshape(rows_block, 3 * share_cols)
    feed_weights = lax.all_gather(feed_rows, "seq", axis=0, tiled=True)
    cot_plane = lax.all_gather(cotangent, "grp", axis=0, tiled=True)
    tok_float = tokens.astype(jnp.float32)
    inverse_one = lax.rsqrt(jnp.mean(tok_float * tok_float, axis=-1, keepdims=True) + NORM_EPS)
    normed = (tok_float * inverse_one * gains[0]).astype(jnp.bfloat16)
    projected = jnp.dot(normed, attn_weights[:, :value_end], preferred_element_type=jnp.float32)
    queries = rotate(projected[:, :query_cols].reshape(rows_here, NH, HD), local_place, 1.0).astype(
        jnp.bfloat16
    )
    key_rows = (
        rotate(
            projected[:, query_cols : query_cols + HD].reshape(rows_here, 1, HD), local_place, 1.0
        )
        .reshape(rows_here, HD)
        .astype(jnp.bfloat16)
    )
    value_rows = projected[:, query_cols + HD : value_end].astype(jnp.bfloat16)
    all_pairs = lax.all_gather(
        jnp.concatenate([key_rows, value_rows], axis=1), "seq", axis=0, tiled=True
    )
    all_keys = all_pairs[:, :HD]
    all_values = all_pairs[:, HD:]
    all_segs = lax.all_gather(segment_ids, "seq", axis=0, tiled=True)
    group_index = jnp.arange(all_keys.shape[0], dtype=jnp.int32)
    group_place = group_index % SEQLEN
    heads_here = NH // seq_count
    head_queries = lax.all_to_all(
        queries.reshape(rows_here, query_cols), "seq", split_axis=1, concat_axis=0, tiled=True
    ).reshape(-1, heads_here, HD)
    head_context, log_totals = attend(
        head_queries, all_keys, all_values, group_index, all_segs, group_index, all_segs
    )
    context = lax.all_to_all(
        head_context.reshape(-1, heads_here * HD).astype(jnp.bfloat16),
        "seq",
        split_axis=0,
        concat_axis=1,
        tiled=True,
    )
    branch = jnp.dot(context, attn_weights[:, value_end:], preferred_element_type=jnp.float32)
    hidden = tok_float + branch
    inverse_two = lax.rsqrt(jnp.mean(hidden * hidden, axis=-1, keepdims=True) + NORM_EPS)
    normed_two = (hidden * inverse_two * gains[1]).astype(jnp.bfloat16)
    normed_plane = lax.all_gather(normed_two, "grp", axis=0, tiled=True)
    gating_weights = feed_weights[:, : 2 * share_cols]
    down_weights = feed_weights[:, 2 * share_cols :]
    gate_up = jnp.dot(normed_plane, gating_weights, preferred_element_type=jnp.float32)
    gate = gate_up[:, :share_cols]
    upper = gate_up[:, share_cols:]
    sigmoid_gate = jax.nn.sigmoid(gate)
    silu_gate = jax.nn.silu(gate)
    activated = (silu_gate * upper).astype(jnp.bfloat16)
    act_grad = jnp.dot(cot_plane, down_weights, preferred_element_type=jnp.float32)
    gate_grad = (act_grad * upper * sigmoid_gate * (1.0 + gate * (1.0 - sigmoid_gate))).astype(
        jnp.bfloat16
    )
    up_grad = (act_grad * silu_gate).astype(jnp.bfloat16)
    gating_grad = jnp.concatenate([gate_grad, up_grad], axis=1)
    norm_two_grad = lax.psum_scatter(
        times_transpose(gating_grad, gating_weights).astype(jnp.bfloat16),
        "grp",
        scatter_dimension=0,
        tiled=True,
    ).astype(jnp.float32)
    feed_grads = jnp.concatenate(
        [contract(normed_plane, gating_grad), contract(cot_plane, activated)], axis=1
    ).astype(jnp.bfloat16)
    feed_grads = lax.psum_scatter(feed_grads, "seq", scatter_dimension=0, tiled=True)
    feed_grads = jnp.transpose(feed_grads.reshape(rows_block, 3 * share, tile_width), (1, 0, 2))
    feed_grads = lax.all_gather(feed_grads, "grp", axis=0, tiled=True)
    feed_out = lax.psum_scatter(
        times_transpose(activated, down_weights).astype(jnp.bfloat16),
        "grp",
        scatter_dimension=0,
        tiled=True,
    ).astype(jnp.float32)
    block_out = (hidden + feed_out).astype(jnp.bfloat16)
    out_grad = cotangent.astype(jnp.float32)
    gain_two_term = jnp.sum(norm_two_grad * hidden * inverse_two, axis=0)
    hidden_grad = (
        out_grad
        + inverse_two * gains[1] * norm_two_grad
        - hidden
        * inverse_two**3
        * jnp.mean(hidden * gains[1] * norm_two_grad, axis=-1, keepdims=True)
    )
    branch_grad = hidden_grad.astype(jnp.bfloat16)
    context_grad = times_transpose(branch_grad, attn_weights[:, value_end:]).astype(jnp.bfloat16)
    head_grads = lax.all_to_all(
        context_grad, "seq", split_axis=1, concat_axis=0, tiled=True
    ).reshape(-1, heads_here, HD)

    def reduce_rows(part):
        cols = part.shape[1]
        blocks = jnp.transpose(
            part.astype(jnp.bfloat16).reshape(seq_count, grp_count, sub_rows, cols), (1, 0, 2, 3)
        ).reshape(grp_count * seq_count * sub_rows, cols)
        summed = lax.psum_scatter(blocks, ("grp", "seq"), scatter_dimension=0, tiled=True)
        return lax.all_gather(summed, "grp", axis=0, tiled=True)

    out_grads = reduce_rows(contract(context, branch_grad))
    head_query_grad, key_part, value_part = attend_back(
        head_queries,
        all_keys,
        all_values,
        head_grads,
        log_totals,
        group_index,
        all_segs,
        group_index,
        all_segs,
    )
    turned_query = (
        rotate(head_query_grad, group_place, -1.0).reshape(-1, heads_here * HD).astype(jnp.bfloat16)
    )
    query_grad = lax.all_to_all(turned_query, "seq", split_axis=0, concat_axis=1, tiled=True)
    key_part = rotate(key_part[:, None, :], group_place, -1.0)[:, 0, :]
    pair_grad = lax.psum_scatter(
        jnp.concatenate([key_part, value_part], axis=1), "seq", scatter_dimension=0, tiled=True
    )
    projected_grad = jnp.concatenate([query_grad, pair_grad.astype(jnp.bfloat16)], axis=1)
    in_grads = reduce_rows(contract(normed, projected_grad))
    norm_one_grad = times_transpose(projected_grad, attn_weights[:, :value_end])
    gain_one_term = jnp.sum(norm_one_grad * tok_float * inverse_one, axis=0)
    input_grad = (
        hidden_grad
        + inverse_one * gains[0] * norm_one_grad
        - tok_float
        * inverse_one**3
        * jnp.mean(tok_float * gains[0] * norm_one_grad, axis=-1, keepdims=True)
    )
    gain_grads = lax.psum(jnp.stack([gain_one_term, gain_two_term]), ("grp", "seq"))
    tile_count = tile_owner_slots.shape[0]
    tile_of_slot = (
        jnp.full((grp_count * slots_here,), tile_count, jnp.int32)
        .at[tile_owner_slots]
        .set(jnp.arange(tile_count, dtype=jnp.int32))
    )
    tiles_here = lax.dynamic_slice_in_dim(tile_of_slot, grp_here * slots_here, slots_here)
    attn_grads = jnp.transpose(
        jnp.concatenate([in_grads, out_grads], axis=1).reshape(rows_block, attn_tiles, tile_width),
        (1, 0, 2),
    )
    feed_at = jnp.clip(tiles_here - attn_tiles, 0, 3 * hidden_tiles - 1)
    which, column = (feed_at // hidden_tiles, feed_at % hidden_tiles)
    feed_at = column // share * (3 * share) + which * share + column % share
    picked = jnp.where(
        (tiles_here < attn_tiles)[:, None, None],
        attn_grads[jnp.minimum(tiles_here, attn_tiles - 1)],
        feed_grads[feed_at],
    )
    reduced_sum = jnp.where((tiles_here < tile_count)[:, None, None], picked, 0).astype(jnp.float32)
    turned = jnp.einsum("zji,zjc->zic", left_basis_set, reduced_sum)
    turned = jnp.einsum("zic,zcd->zid", turned, right_basis_set)
    new_one = BETA_ONE * moment_one + (1.0 - BETA_ONE) * turned
    new_two = BETA_TWO * moment_two + (1.0 - BETA_TWO) * turned * turned
    scaled = new_one / (jnp.sqrt(new_two) + ADAM_EPS)
    restored = jnp.einsum("zij,zjd->zid", left_basis_set, scaled)
    restored = jnp.einsum("zid,zed->zie", restored, right_basis_set)
    new_master = master * (1.0 - LEARN_RATE * WEIGHT_DECAY) - LEARN_RATE * restored
    gain_one = BETA_ONE * gain_moment_one + (1.0 - BETA_ONE) * gain_grads
    gain_two = BETA_TWO * gain_moment_two + (1.0 - BETA_TWO) * gain_grads * gain_grads
    new_gains = gains - GAIN_RATE * gain_one / (jnp.sqrt(gain_two) + ADAM_EPS)
    return (
        block_out,
        input_grad,
        new_master,
        new_one,
        new_two,
        gain_grads,
        new_gains,
        gain_one,
        gain_two,
    )


def solution(mesh):
    return jax.shard_map(
        local,
        mesh=mesh,
        in_specs=(
            P(("grp", "seq"), None),
            P(("grp", "seq"), None),
            P(("grp", "seq")),
            P(),
            P("grp", "seq", None),
            P("grp", "seq", None),
            P("grp", "seq", None),
            P("grp", "seq", None),
            P("grp", "seq", None),
            P("grp", "seq", None),
            P(),
            P(),
            P(),
        ),
        out_specs=(
            P(("grp", "seq"), None),
            P(("grp", "seq"), None),
            P("grp", "seq", None),
            P("grp", "seq", None),
            P("grp", "seq", None),
            P(),
            P(),
            P(),
            P(),
        ),
        check_vma=False,
    )
```

profile of v0, /device:TPU:0, one launch (start us, length us, event | category | flops | bytes accessed | tf_op | source)
XLA Modules:
  0.0 1731.6 jit_solution(6610942294189539147)
XLA Ops:
  8.7 116.0 %all-gather.11.cloned.1.call-done = bf16[168,512,128]{2,1,0:T(8,128)(2,1)} async-done(((bf16[21,512,128]{2,1,0:T(8,128)(2,1)}), bf16[168,512,128]{2,1,0:T(8,128)(2,1)}) %all-gather.11.cloned.1.call-update) | async-done | bytes 22020112 | tf_op jit(solution)/shard_map/all_gather | solution.py:172
  134.4 48.4 %all-gather.13.cloned.1.call-done = bf16[4,64,4352]{2,1,0:T(8,128)(2,1)} async-done(((bf16[1,64,4352]{2,1,0:T(8,128)(2,1)}), bf16[4,64,4352]{2,1,0:T(8,128)(2,1)}) %all-gather.13.cloned.1.call-update) | async-done | bytes 2228240 | tf_op jit(solution)/shard_map/all_gather | solution.py:183
  184.3 10.7 gather_fusion.2
  204.3 73.6 %all-gather.15.cloned.1.call-done = bf16[4,512,4352]{2,1,0:T(8,128)(2,1)} async-done(((bf16[4,64,4352]{2,1,0:T(8,128)(2,1)}), bf16[4,512,4352]{2,1,0:T(8,128)(2,1)}) %all-gather.15.cloned.1.call-update) | async-done | bytes 17825808 | tf_op jit(solution)/shard_map/all_gather | solution.py:184
  277.9 6.3 fusion.83
  296.3 40.8 %all-gather = s32[4,1,256]{2,1,0:T(1,128)S(1)} all-gather(s32[1,1,256]{2,1,0:T(1,128)} %bitcast.336), channel_id=1, replica_groups=mesh['grp'=8,'seq'=4] {'seq'}, dimensions={0}, use_global_device_ids=true | all-gather | bytes 5120 | tf_op jit(solution)/shard_map/all_gather | solution.py:213
  339.6 43.2 %all_gather.37 = bf16[1024,256]{0,1:T(8,128)(2,1)S(1)} all-gather(bf16[256,256]{0,1:T(8,128)(2,1)S(1)} %pad_maximum_fusion.11), channel_id=1, replica_groups=mesh['grp'=8,'seq'=4] {'seq'}, dimensions={0}, use_global_device_ids=true | all-gather | bytes 655360 | tf_op jit(solution)/shard_map/all_gather | solution.py:208
  388.0 17.3 while.36
  410.6 59.3 %all_to_all.61 = bf16[4,256,512]{2,1,0:T(8,128)(2,1)} all-to-all(bf16[4,256,512]{2,1,0:T(8,128)(2,1)} %convert_element_type.137), channel_id=1, replica_groups=mesh['grp'=8,'seq'=4] {'seq'}, dimensions={0} | all-to-all | bytes 2097152 | tf_op jit(solution)/shard_map/all_to_all | solution.py:223
  472.1 6.4 multiply_reduce_fusion
  481.9 18.0 %all-gather.19.cloned.1.call-done = bf16[2048,2304]{0,1:T(8,128)(2,1)} async-done(((bf16[512,2304]{0,1:T(8,128)(2,1)}), bf16[2048,2304]{0,1:T(8,128)(2,1)}) %all-gather.19.cloned.1.call-update) | async-done | bytes 9437200 | tf_op jit(solution)/shard_map/all_gather | solution.py:191
  499.8 54.9 %all-gather.17.cloned.1.call-done = bf16[2048,2048]{1,0:T(8,128)(2,1)} async-done(((bf16[256,2048]{1,0:T(8,128)(2,1)}), bf16[2048,2048]{1,0:T(8,128)(2,1)}) %all-gather.17.cloned.1.call-update) | async-done | bytes 8388624 | tf_op jit(solution)/shard_map/all_gather | solution.py:234
  554.8 19.0 %fusion.95 = f32[2048,1536]{0,1:T(8,128)} fusion(bf16[2048,2048]{1,0:T(8,128)(2,1)} %all-gather.17.cloned.1.call-done, bf16[2048,2304]{0,1:T(8,128)(2,1)} %all-gather.19.cloned.1.call-done), kind=kOutput, calls=%fused_computation.134 | convolution fusion | flops 12884901888 | bytes 27262976 | tf_op jit(solution)/shard_map/dot_general | solution.py:237
  573.7 37.2 %all-gather.21.cloned.1.call-done = bf16[2048,2048]{1,0:T(8,128)(2,1)} async-done(((bf16[256,2048]{1,0:T(8,128)(2,1)}), bf16[2048,2048]{1,0:T(8,128)(2,1)}) %all-gather.21.cloned.1.call-update) | async-done | bytes 8388624 | tf_op jit(solution)/shard_map/all_gather | solution.py:192
  610.9 16.7 fusion.91
  629.3 18.7 %convolution_convert_fusion.3 = bf16[2048,2048]{1,0:T(8,128)(2,1)} fusion(bf16[2048,2304]{0,1:T(8,128)(2,1)} %all-gather.19.cloned.1.call-done, bf16[2048,768]{0,1:T(8,128)(2,1)} %get-tuple-element.680, bf16[2048,768]{0,1:T(8,128)(2,1)S(1)} %get-tuple-element.679), kind=kOutput, calls=%fused_computation.117 | convolution fusion | flops 12901679104 | bytes 20971520 | tf_op jit(solution)/shard_map/dot_general | solution.py:51
  648.1 11.9 convolution_convert_fusion.4
  660.0 59.5 %reduce-scatter.9.cloned.1.call-done = bf16[256,2048]{1,0:T(8,128)(2,1)} async-done(((bf16[2048,2048]{1,0:T(8,128)(2,1)}), bf16[256,2048]{1,0:T(8,128)(2,1)}) %reduce-scatter.9.cloned.1.call-update) | async-done | bytes 1048592 | tf_op jit(solution)/shard_map/reduce_scatter | solution.py:249
  722.5 72.2 %reduce-scatter.7.cloned.1.call-done = bf16[256,2048]{1,0:T(8,128)(2,1)} async-done(((bf16[2048,2048]{1,0:T(8,128)(2,1)}), bf16[256,2048]{1,0:T(8,128)(2,1)}) %reduce-scatter.7.cloned.1.call-update) | async-done | bytes 1048592 | tf_op jit(solution)/shard_map/reduce_scatter | solution.py:261
  798.9 6.5 fusion.114
  811.1 25.8 %all-to-all-done.2 = bf16[256,4,512]{2,0,1:T(8,128)(2,1)} async-done(((bf16[256,4,512]{2,0,1:T(8,128)(2,1)}), bf16[256,4,512]{2,0,1:T(8,128)(2,1)}, u32[]{:S(2)}, u32[]{:S(2)}) %all-to-all-start.2) | async-done | bytes 1048608 | tf_op jit(solution)/shard_map/all_to_all | solution.py:279
  839.5 123.5 %while.37 = (s32[]{:T(128)}, f32[1024,128]{1,0:T(8,128)}, f32[1024,128]{1,0:T(8,128)}, f32[2,512,4,128]{3,1,0,2:T(8,128)}, s32[2,512]{1,0:T(2,128)S(1)}, /*index...) while((s32[]{:T(128)}, f32[1024,128]{1,0:T(8,128)}, ...), condition=%wide.region_11.12_spmd.clone.clone, body=%wide.region_9.11_spmd.clone.clone.sunk | while | flops 2742048256 | bytes 106783928 | solution.py:128
  850.3 22.8 %fusion.228 = f32[2,512,4,128]{3,1,0,2:T(8,128)} fusion(f32[2,512,4,128]{3,1,0,2:T(8,128)} %get-tuple-element.900, s32[]{:T(128)} %get-tuple-element.897, f32[512,4,1024]{2,0,1:T(8,128)} %fusion.223, f32[512,4,1024]{2,0,1:T(8,128)} %fusion.224, f32[4,512]{1,0:T(4,128)S(1)} %dynamic-slice_bitcast_fusion.2, pred[512,1024]{1,0:T(8,128)(4,1)} %fusion.225, ...), kind=kOutput, calls=%fused_computation.67.clone.1 | convolution fusion | flops 559942656 | bytes 35930624 | tf_op jit(solution)/shard_map/while/body/eval_jaxpr/hqk,kd->qhd/dot_general | solution.py:113
  873.1 21.3 %fusion.226 = f32[1024,128]{1,0:T(8,128)} fusion(f32[512,4,1024]{2,0,1:T(8,128)} %fusion.223, f32[512,4,1024]{2,0,1:T(8,128)} %fusion.224, f32[4,512]{1,0:T(4,128)S(1)} %dynamic-slice_bitcast_fusion.2, pred[512,1024]{1,0:T(8,128)(4,1)} %fusion.225, f32[1024,128]{1,0:T(8,128)} %get-tuple-element.898, ...), kind=kOutput, calls=%fused_computation.70.clone.1 | convolution fusion | flops 560204800 | bytes 36192768 | tf_op jit(solution)/shard_map/while/body/eval_jaxpr/hqk,qhd->kd/dot_general | solution.py:116
  894.4 6.7 fusion.227
  912.0 22.8 %fusion.228 = f32[2,512,4,128]{3,1,0,2:T(8,128)} fusion(f32[2,512,4,128]{3,1,0,2:T(8,128)} %get-tuple-element.900, s32[]{:T(128)} %get-tuple-element.897, f32[512,4,1024]{2,0,1:T(8,128)} %fusion.223, f32[512,4,1024]{2,0,1:T(8,128)} %fusion.224, f32[4,512]{1,0:T(4,128)S(1)} %dynamic-slice_bitcast_fusion.2, pred[512,1024]{1,0:T(8,128)(4,1)} %fusion.225, ...), kind=kOutput, calls=%fused_computation.67.clone.1 | convolution fusion | flops 559942656 | bytes 35930624 | tf_op jit(solution)/shard_map/while/body/eval_jaxpr/hqk,kd->qhd/dot_general | solution.py:113
  934.8 21.3 %fusion.226 = f32[1024,128]{1,0:T(8,128)} fusion(f32[512,4,1024]{2,0,1:T(8,128)} %fusion.223, f32[512,4,1024]{2,0,1:T(8,128)} %fusion.224, f32[4,512]{1,0:T(4,128)S(1)} %dynamic-slice_bitcast_fusion.2, pred[512,1024]{1,0:T(8,128)(4,1)} %fusion.225, f32[1024,128]{1,0:T(8,128)} %get-tuple-element.898, ...), kind=kOutput, calls=%fused_computation.70.clone.1 | convolution fusion | flops 560204800 | bytes 36192768 | tf_op jit(solution)/shard_map/while/body/eval_jaxpr/hqk,qhd->kd/dot_general | solution.py:116
  956.1 6.9 fusion.227
  977.2 41.2 %all_to_all.62 = bf16[4,256,512]{2,1,0:T(8,128)(2,1)} all-to-all(bf16[4,256,512]{2,1,0:T(8,128)(2,1)} %convert_element_type.151), channel_id=1, replica_groups=mesh['grp'=8,'seq'=4] {'seq'}, dimensions={0} | all-to-all | bytes 2097152 | tf_op jit(solution)/shard_map/all_to_all | solution.py:306
  1021.1 5.3 convolution_convert_fusion
  1026.4 8.3 copy.118
  1036.3 6.9 convolution_convert_fusion.2
  1043.1 8.7 copy.119
  1052.0 10.8 fusion.102
  1062.7 15.9 convolution_convert_fusion.1
  1078.6 11.5 pad_maximum_fusion
  1090.2 79.3 %reduce-scatter.13.cloned.1.call-done = bf16[64,2304]{1,0:T(8,128)(2,1)} async-done(((bf16[2048,2304]{1,0:T(8,128)(2,1)}), bf16[64,2304]{1,0:T(8,128)(2,1)}) %reduce-scatter.13.cloned.1.call-update) | async-done | bytes 294928 | tf_op jit(solution)/shard_map/reduce_scatter | solution.py:288
  1169.6 187.0 %reduce-scatter.15.cloned.1.call-done = bf16[64,2048]{1,0:T(8,128)(2,1)} async-done(((bf16[2048,2048]{1,0:T(8,128)(2,1)}), bf16[64,2048]{1,0:T(8,128)(2,1)}) %reduce-scatter.15.cloned.1.call-update) | async-done | bytes 262160 | tf_op jit(solution)/shard_map/reduce_scatter | solution.py:288
  1356.7 161.1 %reduce-scatter.17.cloned.1.call-done = bf16[512,2304]{0,1:T(8,128)(2,1)} async-done(((bf16[2048,2304]{0,1:T(8,128)(2,1)}), bf16[512,2304]{0,1:T(8,128)(2,1)}) %reduce-scatter.17.cloned.1.call-update) | async-done | bytes 2359312 | tf_op jit(solution)/shard_map/reduce_scatter | solution.py:258
  1525.1 9.3 fusion.133
  1534.5 41.6 %psum.7 = f32[2,2048]{1,0:T(2,128)S(1)} all-reduce(f32[2,2048]{1,0:T(2,128)S(1)} %pad_maximum_fusion.12), channel_id=1, replica_groups=mesh['grp'=8,'seq'=4] {'grp','seq'}, use_global_device_ids=true, to_apply=%region_20.21 | all-reduce | flops 4096 | bytes 32768 | tf_op jit(solution)/shard_map/psum | solution.py:322
  1586.7 6.7 copy.120
  1593.4 6.7 copy.121
  1600.1 5.0 gather_fusion.3
  1605.0 76.1 %all-gather.27.cloned.1.call-done = bf16[144,512,128]{2,1,0:T(8,128)(2,1)} async-done(((bf16[18,512,128]{2,1,0:T(8,128)(2,1)}), bf16[144,512,128]{2,1,0:T(8,128)(2,1)}) %all-gather.27.cloned.1.call-update) | async-done | bytes 18874384 | tf_op jit(solution)/shard_map/all_gather | solution.py:260
  1681.1 8.9 gather_fusion.4
  1690.0 18.5 %fusion.97 = (f32[21,512,128]{2,1,0:T(8,128)}, f32[21,512,128]{2,1,0:T(8,128)}) fusion(f32[21,512,128]{2,1,0:T(8,128)} %param.24, f32[21,512,128]{2,1,0:T(8,128)} %param.23, f32[21,128,128]{2,1,0:T(8,128)S(1)} %copy-done, f32[21,512,512]{2,1,0:T(8,128)} %param.25, bf16[21,512,128]{2,1,0:T(8,128)(2,1)} %gather_fusion.3, ...), kind=kOutput, calls=%fused_computation.136 | convolution fusion | flops 1772617728 | bytes 50921512 | tf_op jit(solution)/shard_map/zic,zcd->zid/dot_general | solution.py:344
  1708.5 16.1 multiply_subtract_fusion
  (219 shorter events, 145.0 us)
Async XLA Ops:
  7.2 1682.9 %copy-start = (f32[21,128,128]{2,1,0:T(8,128)S(1)}, f32[21,128,128]{2,1,0:T(8,128)}, u32[]{:S(2)}) copy-start(f32[21,128,128]{2,1,0:T(8,128)} %param.26) | copy-start | bytes 4128772
  7.2 117.5 %all-gather.11.cloned.1.call-start = ((), (), s32[]{:S(2)}) async-start(), calls=%async_computation.10 | async-start | bytes 24772608 | tf_op jit(solution)/shard_map/all_gather | solution.py:172
  7.9 174.9 %all-gather.13.cloned.1.call-start = ((), (), s32[]{:S(2)}) async-start(), calls=%async_computation.11 | async-start | bytes 2785280 | tf_op jit(solution)/shard_map/all_gather | solution.py:183
  8.7 174.4 %copy-start.1 = (s32[166]{0:T(256)S(1)}, s32[166]{0:T(256)}, u32[]{:S(2)}) copy-start(s32[166]{0:T(256)} %param.20) | copy-start | bytes 1996
  8.7 175.3 %copy-start.7 = (bf16[256,2048]{1,0:T(8,128)(2,1)S(1)}, bf16[256,2048]{1,0:T(8,128)(2,1)}, u32[]{:S(2)}) copy-start(bf16[256,2048]{1,0:T(8,128)(2,1)} %param.17) | copy-start | bytes 3145732
  134.4 143.5 %all-gather.15.cloned.1.call-start = ((), (), s32[]{:S(2)}) async-start(), calls=%async_computation.12 | async-start | bytes 20054016 | tf_op jit(solution)/shard_map/all_gather | solution.py:184
  182.9 317.0 %all-gather.19.cloned.1.call-start = ((), (), s32[]{:S(2)}) async-start(), calls=%async_computation.14 | async-start | bytes 11796480 | tf_op jit(solution)/shard_map/all_gather | solution.py:191
  194.9 9.3 copy-start.15
  202.7 136.5 %copy-start.22 = (f32[64]{0:T(128)}, f32[64]{0:T(128)S(1)}, u32[]{:S(2)}) copy-start(f32[64]{0:T(128)S(1)} %multiply_power_fusion) | copy-start | bytes 772
  203.3 80.9 %copy-start.19 = (f32[256]{0:T(256)}, f32[256]{0:T(256)S(1)}, u32[]{:S(2)}) copy-start(f32[256]{0:T(256)S(1)} %get-tuple-element.703) | copy-start | bytes 3076
  204.3 80.0 %copy-start.13 = (f32[1,2048]{1,0:T(1,128)}, f32[1,2048]{1,0:T(1,128)S(1)}, u32[]{:S(2)}) copy-start(f32[1,2048]{1,0:T(1,128)S(1)} %get-tuple-element.697) | copy-start | bytes 24580
  284.3 1.4 copy-start.11
  291.7 91.5 %all-to-all-start = ((bf16[256,4,512]{0,2,1:T(8,128)(2,1)}), bf16[256,4,512]{0,2,1:T(8,128)(2,1)S(1)}, u32[]{:S(2)}, u32[]{:S(2)}) async-start(bf16[256,4,512]{0,2,1:T(8,128)(2,1)} %bitcast.5), calls=%async_computation | async-start | bytes 2097152 | tf_op jit(solution)/shard_map/all_to_all | solution.py:217
  296.3 258.4 %all-gather.17.cloned.1.call-start = ((), (), s32[]{:S(2)}) async-start(), calls=%async_computation.13 | async-start | bytes 9437184 | tf_op jit(solution)/shard_map/all_gather | solution.py:234
  478.5 1.3 copy-start.5
  481.1 129.9 %all-gather.21.cloned.1.call-start = ((), (), s32[]{:S(2)}) async-start(), calls=%async_computation.16 | async-start | bytes 9437184 | tf_op jit(solution)/shard_map/all_gather | solution.py:192
  481.7 237.9 %reduce-scatter.9.cloned.1.call-start = ((), (), s32[]{:S(2)}) async-start(), calls=%async_computation.17 | async-start | bytes 9437184 | tf_op jit(solution)/shard_map/reduce_scatter | solution.py:249
  627.6 1.7 copy-start.26
  648.1 146.6 %reduce-scatter.7.cloned.1.call-start = ((), (), s32[]{:S(2)}) async-start(), calls=%async_computation.15 | async-start | bytes 9437184 | tf_op jit(solution)/shard_map/reduce_scatter | solution.py:261
  798.9 6.5 copy-start.3
  806.5 30.4 %all-to-all-start.2 = ((bf16[256,4,512]{2,0,1:T(8,128)(2,1)}), bf16[256,4,512]{2,0,1:T(8,128)(2,1)}, u32[]{:S(2)}, u32[]{:S(2)}) async-start(bf16[256,4,512]{2,0,1:T(8,128)(2,1)} %bitcast.312), calls=%async_computation.4 | async-start | bytes 2097152 | tf_op jit(solution)/shard_map/all_to_all | solution.py:279
  811.1 208.7 %reduce-scatter.11.cloned.1.call-start = ((), (), s32[]{:S(2)}) async-start(), calls=%async_computation.18 | async-start | bytes 1310720 | tf_op jit(solution)/shard_map/reduce_scatter | solution.py:308
  839.5 127.7 %copy-start.23 = (f32[64]{0:T(128)S(1)}, f32[64]{0:T(128)}, u32[]{:S(2)}) copy-start(f32[64]{0:T(128)} %copy-done.22) | copy-start | bytes 772
  839.5 6.1 copy-start.6
  901.2 6.1 copy-start.6
  963.0 10.7 copy-start.9
  971.8 197.8 %reduce-scatter.13.cloned.1.call-start = ((), (), s32[]{:S(2)}) async-start(), calls=%async_computation.19 | async-start | bytes 9732096 | tf_op jit(solution)/shard_map/reduce_scatter | solution.py:288
  974.5 46.6 %copy-start.8 = (bf16[256,2048]{1,0:T(8,128)(2,1)S(1)}, bf16[256,2048]{1,0:T(8,128)(2,1)}, u32[]{:S(2)}) copy-start(bf16[256,2048]{1,0:T(8,128)(2,1)} %param.17) | copy-start | bytes 3145732
  974.5 46.6 %copy-start.14 = (f32[1,2048]{1,0:T(1,128)S(1)}, f32[1,2048]{1,0:T(1,128)}, u32[]{:S(2)}) copy-start(f32[1,2048]{1,0:T(1,128)} %copy-done.13) | copy-start | bytes 24580
  974.5 46.6 %copy-start.20 = (f32[256]{0:T(256)S(1)}, f32[256]{0:T(256)}, u32[]{:S(2)}) copy-start(f32[256]{0:T(256)} %copy-done.19) | copy-start | bytes 3076
  1019.8 6.6 copy-start.10
  1021.0 5.4 copy-start.12
  1034.7 1.6 copy-start.4
  1034.7 321.9 %reduce-scatter.15.cloned.1.call-start = ((), (), s32[]{:S(2)}) async-start(), calls=%async_computation.21 | async-start | bytes 8650752 | tf_op jit(solution)/shard_map/reduce_scatter | solution.py:288
  1051.9 465.9 %reduce-scatter.17.cloned.1.call-start = ((), (), s32[]{:S(2)}) async-start(), calls=%async_computation.23 | async-start | bytes 11796480 | tf_op jit(solution)/shard_map/reduce_scatter | solution.py:258
  1051.9 10.8 copy-start.27
  1052.0 10.8 copy-start.28
  1090.1 432.0 %copy-start.2 = (s32[166]{0:T(256)S(1)}, s32[166]{0:T(256)}, u32[]{:S(2)}) copy-start(s32[166]{0:T(256)} %param.20) | copy-start | bytes 1996
  1090.2 491.9 %all-gather.23.cloned.1.call-start = ((), (), s32[]{:S(2)}) async-start(), calls=%async_computation.20 | async-start | bytes 2654208 | tf_op jit(solution)/shard_map/all_gather | solution.py:289
  1169.5 412.5 %all-gather.25.cloned.1.call-start = ((), (), s32[]{:S(2)}) async-start(), calls=%async_computation.22 | async-start | bytes 2359296 | tf_op jit(solution)/shard_map/all_gather | solution.py:289
  1356.6 324.5 %all-gather.27.cloned.1.call-start = ((), (), s32[]{:S(2)}) async-start(), calls=%async_computation.24 | async-start | bytes 21233664 | tf_op jit(solution)/shard_map/all_gather | solution.py:260
  1525.1 9.3 copy-start.18
  1525.1 51.6 %copy-start.16 = (f32[2,2048]{1,0:T(2,128)S(1)}, f32[2,2048]{1,0:T(2,128)}, u32[]{:S(2)}) copy-start(f32[2,2048]{1,0:T(2,128)} %param.27) | copy-start | bytes 49156
  1525.1 51.6 %copy-start.21 = (f32[2,2048]{1,0:T(2,128)S(1)}, f32[2,2048]{1,0:T(2,128)}, u32[]{:S(2)}) copy-start(f32[2,2048]{1,0:T(2,128)} %param.28) | copy-start | bytes 49156
  1576.1 10.7 copy-start.17
  1600.1 90.0 %copy-start.24 = (pred[21]{0:T(512)(128)(4,1)S(1)}, pred[21]{0:T(512)(128)(4,1)}, u32[]{:S(2)}) copy-start(pred[21]{0:T(512)(128)(4,1)} %get-tuple-element.671) | copy-start | bytes 67
  1600.1 90.0 %copy-start.25 = (pred[21]{0:T(512)(128)(4,1)S(1)}, pred[21]{0:T(512)(128)(4,1)}, u32[]{:S(2)}) copy-start(pred[21]{0:T(512)(128)(4,1)} %broadcast_compare_fusion) | copy-start | bytes 67
Sparse Core Ops, SparseCore 0:
  9.9 114.7 all-gather.10
  134.5 48.3 all-gather.12
  184.8 93.1 all-gather.14
  279.9 219.8 all-gather.18
  502.1 52.5 all-gather.16
  556.5 54.3 all-gather.20
  648.2 71.2 reduce-scatter.8
  723.4 71.2 reduce-scatter.6
  971.9 35.7 reduce-scatter.10
  1034.8 134.6 reduce-scatter.12
  1171.8 184.7 reduce-scatter.14
  1358.8 158.9 reduce-scatter.16
  1519.7 30.3 all-gather.22
  1551.9 28.3 all-gather.24
  1582.5 98.5 all-gather.26
where the time goes:
time: 1740 us; the launch traced here: 1730 us
  waiting for transfers between devices  1010 us (58%)
  matrix products  299 us (17%)
  blocking collectives  226 us (13%)
  local copies, waits for them, and re-layouts  112 us (6%)
  other arithmetic  59.6 us (3%)
    reduce_scatter x2, waiting for transfers between devices, reduce_rows(): lax.psum_scatter(blocks, ('grp', 'seq'), scatter_dimension=0, tiled=True)  266 us
    reduce_scatter x1, waiting for transfers between devices, local(): lax.psum_scatter(feed_grads, 'seq', scatter_dimension=0, tiled=True)  161 us
    all_gather x1, waiting for transfers between devices, local(): plane_tiles = lax.all_gather(weights_low, 'grp', axis=0, tiled=True)  116 us
    all_gather x1, waiting for transfers between devices, local(): feed_grads = lax.all_gather(feed_grads, 'grp', axis=0, tiled=True)  76.1 us
    all_gather x1, waiting for transfers between devices, local(): lax.all_gather(attn_weights, 'grp', axis=1, tiled=True)  73.6 us
    reduce_scatter x1, waiting for transfers between devices, local(): lax.psum_scatter(times_transpose(activated, down_weights).astype(jnp.bflo...  72.2 us
    reduce_scatter x1, waiting for transfers between devices, local(): lax.psum_scatter(times_transpose(gating_grad, gating_weights).astype(jnp....  59.5 us
    all_to_all x1, blocking collectives, local(): lax.all_to_all(head_context.reshape(-1, heads_here * HD).astype(jnp.bfloa...  59.3 us
  transfers between devices with their start and end apart: 17, of which 13 were waited for; matrix products, arithmetic and copies ran while one was open for 12% of the time, Pallas kernels for 0%

commit v1 on v0

--- a/solution.py
+++ b/solution.py
@@ -18,6 +18,35 @@
 ROPE_BASE = 10000.0
 MASKED = -1e30
 PRECISE = lax.Precision.HIGHEST
+
+
+def convert_ticks_on(vec, axis_k, point):
+    reply = vec.shape
+    ready = vec.reshape(*reply[:axis_k], point, reply[axis_k] // point, *reply[axis_k + 1 :])
+    return jnp.moveaxis(ready, axis_k, 0)
+
+
+def advance_row(local_block, row_dim):
+    local_block = jnp.moveaxis(local_block, 0, row_dim)
+    main = local_block.shape
+    return local_block.reshape(
+        *main[:row_dim], main[row_dim] * main[row_dim + 1], *main[row_dim + 2 :]
+    )
+
+
+def body_update(shard_in, across, in_array, array_in):
+    big = lax.axis_size(across)
+    block_last = lax.axis_index(across)
+    answer, p_next = (big, block_last)
+    a_next = convert_ticks_on(shard_in, in_array, answer)
+    runs = [a_next[p_next]]
+    for dd in range(1, answer):
+        h_now = a_next[p_next ^ dd]
+        s_next = lax.ppermute(h_now, axis_name=across, perm=[(j0, j0 ^ dd) for j0 in range(answer)])
+        runs.append(s_next)
+    current_block = jnp.stack(runs)
+    a_next = current_block[p_next ^ jnp.arange(answer)]
+    return advance_row(a_next, array_in)
 
 
 def rotate(values, positions, direction):
@@ -303,7 +332,7 @@
     turned_query = (
         rotate(head_query_grad, group_place, -1.0).reshape(-1, heads_here * HD).astype(jnp.bfloat16)
     )
-    query_grad = lax.all_to_all(turned_query, "seq", split_axis=0, concat_axis=1, tiled=True)
+    query_grad = body_update(turned_query, "seq", 0, 1)
     key_part = rotate(key_part[:, None, :], group_place, -1.0)[:, 0, :]
     pair_grad = lax.psum_scatter(
         jnp.concatenate([key_part, value_part], axis=1), "seq", scatter_dimension=0, tiled=True

time: 1740 us -> 1740 us (level)
  blocking collectives: 226 us -> 185 us
  waiting for transfers between devices: 1010 us -> 1050 us
    all_to_all x1 -> x0, blocking collectives: 41.2 us -> none  [local(): lax.all_to_all(turned_query, 'seq', split_axis=0, concat_axis=1, tiled=True)]
    ppermute x0 -> x3, waiting for transfers between devices: none -> 30.3 us  [body_update(): lax.ppermute(h_now, axis_name=across, perm=[(j0, j0 ^ dd) for j0 in range...]
  transfers between devices with their start and end apart: 17 -> 20, of which waited for: 13 -> 15; matrix products, arithmetic and copies ran while one was open for 12% -> 13% of each run, Pallas kernels for 0% -> 0%
where the time goes in v1:
time: 1740 us; the launch traced here: 1730 us
  waiting for transfers between devices  1050 us (60%)
  matrix products  299 us (17%)
  blocking collectives  185 us (11%)
  local copies, waits for them, and re-layouts  115 us (7%)
  other arithmetic  59.6 us (3%)
    reduce_scatter x2, waiting for transfers between devices, reduce_rows(): lax.psum_scatter(blocks, ('grp', 'seq'), scatter_dimension=0, tiled=True)  270 us
    reduce_scatter x1, waiting for transfers between devices, local(): lax.psum_scatter(feed_grads, 'seq', scatter_dimension=0, tiled=True)  161 us
    all_gather x1, waiting for transfers between devices, local(): plane_tiles = lax.all_gather(weights_low, 'grp', axis=0, tiled=True)  116 us
    all_gather x1, waiting for transfers between devices, local(): feed_grads = lax.all_gather(feed_grads, 'grp', axis=0, tiled=True)  76.3 us
    all_gather x1, waiting for transfers between devices, local(): lax.all_gather(attn_weights, 'grp', axis=1, tiled=True)  73.6 us
    reduce_scatter x1, waiting for transfers between devices, local(): lax.psum_scatter(times_transpose(activated, down_weights).astype(jnp.bflo...  72.2 us
    reduce_scatter x1, waiting for transfers between devices, local(): lax.psum_scatter(times_transpose(gating_grad, gating_weights).astype(jnp....  59.5 us
    all_to_all x1, blocking collectives, local(): lax.all_to_all(head_context.reshape(-1, heads_here * HD).astype(jnp.bfloa...  59.3 us
  transfers between devices with their start and end apart: 20, of which 15 were waited for; matrix products, arithmetic and copies ran while one was open for 13% of the time, Pallas kernels for 0%

profile of v1, /device:TPU:0, one launch (start us, length us, event | category | flops | bytes accessed | tf_op | source)
XLA Modules:
  0.0 1732.2 jit_solution(11586407400879836406)
XLA Ops:
  8.7 116.0 %all-gather.11.cloned.1.call-done = bf16[168,512,128]{2,1,0:T(8,128)(2,1)} async-done(((bf16[21,512,128]{2,1,0:T(8,128)(2,1)}), bf16[168,512,128]{2,1,0:T(8,128)(2,1)}) %all-gather.11.cloned.1.call-update) | async-done | bytes 22020112 | tf_op jit(solution)/shard_map/all_gather | solution.py:201
  134.4 48.4 %all-gather.13.cloned.1.call-done = bf16[4,64,4352]{2,1,0:T(8,128)(2,1)} async-done(((bf16[1,64,4352]{2,1,0:T(8,128)(2,1)}), bf16[4,64,4352]{2,1,0:T(8,128)(2,1)}) %all-gather.13.cloned.1.call-update) | async-done | bytes 2228240 | tf_op jit(solution)/shard_map/all_gather | solution.py:212
  184.3 10.7 gather_fusion.2
  204.3 73.6 %all-gather.15.cloned.1.call-done = bf16[4,512,4352]{2,1,0:T(8,128)(2,1)} async-done(((bf16[4,64,4352]{2,1,0:T(8,128)(2,1)}), bf16[4,512,4352]{2,1,0:T(8,128)(2,1)}) %all-gather.15.cloned.1.call-update) | async-done | bytes 17825808 | tf_op jit(solution)/shard_map/all_gather | solution.py:213
  277.9 6.3 fusion.83
  296.3 40.8 %all-gather = s32[4,1,256]{2,1,0:T(1,128)S(1)} all-gather(s32[1,1,256]{2,1,0:T(1,128)} %bitcast.350), channel_id=1, replica_groups=mesh['grp'=8,'seq'=4] {'seq'}, dimensions={0}, use_global_device_ids=true | all-gather | bytes 5120 | tf_op jit(solution)/shard_map/all_gather | solution.py:242
  339.6 43.2 %all_gather.37 = bf16[1024,256]{0,1:T(8,128)(2,1)S(1)} all-gather(bf16[256,256]{0,1:T(8,128)(2,1)S(1)} %pad_maximum_fusion.12), channel_id=1, replica_groups=mesh['grp'=8,'seq'=4] {'seq'}, dimensions={0}, use_global_device_ids=true | all-gather | bytes 655360 | tf_op jit(solution)/shard_map/all_gather | solution.py:237
  388.0 17.3 while.36
  410.6 59.3 %all_to_all.45 = bf16[4,256,512]{2,1,0:T(8,128)(2,1)} all-to-all(bf16[4,256,512]{2,1,0:T(8,128)(2,1)} %convert_element_type.137), channel_id=1, replica_groups=mesh['grp'=8,'seq'=4] {'seq'}, dimensions={0} | all-to-all | bytes 2097152 | tf_op jit(solution)/shard_map/all_to_all | solution.py:252
  472.2 6.4 multiply_reduce_fusion
  481.9 18.0 %all-gather.19.cloned.1.call-done = bf16[2048,2304]{0,1:T(8,128)(2,1)} async-done(((bf16[512,2304]{0,1:T(8,128)(2,1)}), bf16[2048,2304]{0,1:T(8,128)(2,1)}) %all-gather.19.cloned.1.call-update) | async-done | bytes 9437200 | tf_op jit(solution)/shard_map/all_gather | solution.py:220
  499.8 54.9 %all-gather.17.cloned.1.call-done = bf16[2048,2048]{1,0:T(8,128)(2,1)} async-done(((bf16[256,2048]{1,0:T(8,128)(2,1)}), bf16[2048,2048]{1,0:T(8,128)(2,1)}) %all-gather.17.cloned.1.call-update) | async-done | bytes 8388624 | tf_op jit(solution)/shard_map/all_gather | solution.py:263
  554.8 19.0 %fusion.95 = f32[2048,1536]{0,1:T(8,128)} fusion(bf16[2048,2048]{1,0:T(8,128)(2,1)} %all-gather.17.cloned.1.call-done, bf16[2048,2304]{0,1:T(8,128)(2,1)} %all-gather.19.cloned.1.call-done), kind=kOutput, calls=%fused_computation.135 | convolution fusion | flops 12884901888 | bytes 27262976 | tf_op jit(solution)/shard_map/dot_general | solution.py:266
  573.7 37.2 %all-gather.21.cloned.1.call-done = bf16[2048,2048]{1,0:T(8,128)(2,1)} async-done(((bf16[256,2048]{1,0:T(8,128)(2,1)}), bf16[2048,2048]{1,0:T(8,128)(2,1)}) %all-gather.21.cloned.1.call-update) | async-done | bytes 8388624 | tf_op jit(solution)/shard_map/all_gather | solution.py:221
  610.9 16.7 fusion.91
  629.3 18.8 %convolution_convert_fusion.3 = bf16[2048,2048]{1,0:T(8,128)(2,1)} fusion(bf16[2048,2304]{0,1:T(8,128)(2,1)} %all-gather.19.cloned.1.call-done, bf16[2048,768]{0,1:T(8,128)(2,1)} %get-tuple-element.680, bf16[2048,768]{0,1:T(8,128)(2,1)S(1)} %get-tuple-element.679), kind=kOutput, calls=%fused_computation.118 | convolution fusion | flops 12901679104 | bytes 20971520 | tf_op jit(solution)/shard_map/dot_general | solution.py:80
  648.1 11.9 convolution_convert_fusion.4
  660.0 59.5 %reduce-scatter.9.cloned.1.call-done = bf16[256,2048]{1,0:T(8,128)(2,1)} async-done(((bf16[2048,2048]{1,0:T(8,128)(2,1)}), bf16[256,2048]{1,0:T(8,128)(2,1)}) %reduce-scatter.9.cloned.1.call-update) | async-done | bytes 1048592 | tf_op jit(solution)/shard_map/reduce_scatter | solution.py:278
  722.5 72.2 %reduce-scatter.7.cloned.1.call-done = bf16[256,2048]{1,0:T(8,128)(2,1)} async-done(((bf16[2048,2048]{1,0:T(8,128)(2,1)}), bf16[256,2048]{1,0:T(8,128)(2,1)}) %reduce-scatter.7.cloned.1.call-update) | async-done | bytes 1048592 | tf_op jit(solution)/shard_map/reduce_scatter | solution.py:290
  798.9 6.5 fusion.114
  811.2 25.8 %all-to-all-done.2 = bf16[256,4,512]{2,0,1:T(8,128)(2,1)} async-done(((bf16[256,4,512]{2,0,1:T(8,128)(2,1)}), bf16[256,4,512]{2,0,1:T(8,128)(2,1)}, u32[]{:S(2)}, u32[]{:S(2)}) %all-to-all-start.2) | async-done | bytes 1048608 | tf_op jit(solution)/shard_map/all_to_all | solution.py:308
  839.6 123.2 %while.37 = (s32[]{:T(128)}, f32[1024,128]{1,0:T(8,128)}, f32[1024,128]{1,0:T(8,128)}, f32[2,512,4,128]{3,1,0,2:T(8,128)}, s32[2,512]{1,0:T(2,128)S(1)}, /*index...) while((s32[]{:T(128)}, f32[1024,128]{1,0:T(8,128)}, ...), condition=%wide.region_11.12_spmd.clone.clone, body=%wide.region_9.11_spmd.clone.clone.sunk | while | flops 2742048256 | bytes 106783928 | solution.py:157
  850.4 22.8 %fusion.229 = f32[2,512,4,128]{3,1,0,2:T(8,128)} fusion(f32[2,512,4,128]{3,1,0,2:T(8,128)} %get-tuple-element.904, s32[]{:T(128)} %get-tuple-element.901, f32[512,4,1024]{2,0,1:T(8,128)} %fusion.224, f32[512,4,1024]{2,0,1:T(8,128)} %fusion.225, f32[4,512]{1,0:T(4,128)S(1)} %dynamic-slice_bitcast_fusion.5, pred[512,1024]{1,0:T(8,128)(4,1)} %fusion.226, ...), kind=kOutput, calls=%fused_computation.68.clone.1 | convolution fusion | flops 559942656 | bytes 35930624 | tf_op jit(solution)/shard_map/while/body/eval_jaxpr/hqk,kd->qhd/dot_general | solution.py:142
  873.2 21.1 %fusion.227 = f32[1024,128]{1,0:T(8,128)} fusion(f32[512,4,1024]{2,0,1:T(8,128)} %fusion.224, f32[512,4,1024]{2,0,1:T(8,128)} %fusion.225, f32[4,512]{1,0:T(4,128)S(1)} %dynamic-slice_bitcast_fusion.5, pred[512,1024]{1,0:T(8,128)(4,1)} %fusion.226, f32[1024,128]{1,0:T(8,128)} %get-tuple-element.902, ...), kind=kOutput, calls=%fused_computation.71.clone.1 | convolution fusion | flops 560204800 | bytes 36192768 | tf_op jit(solution)/shard_map/while/body/eval_jaxpr/hqk,qhd->kd/dot_general | solution.py:145
  894.3 6.8 fusion.228
  911.9 22.8 %fusion.229 = f32[2,512,4,128]{3,1,0,2:T(8,128)} fusion(f32[2,512,4,128]{3,1,0,2:T(8,128)} %get-tuple-element.904, s32[]{:T(128)} %get-tuple-element.901, f32[512,4,1024]{2,0,1:T(8,128)} %fusion.224, f32[512,4,1024]{2,0,1:T(8,128)} %fusion.225, f32[4,512]{1,0:T(4,128)S(1)} %dynamic-slice_bitcast_fusion.5, pred[512,1024]{1,0:T(8,128)(4,1)} %fusion.226, ...), kind=kOutput, calls=%fused_computation.68.clone.1 | convolution fusion | flops 559942656 | bytes 35930624 | tf_op jit(solution)/shard_map/while/body/eval_jaxpr/hqk,kd->qhd/dot_general | solution.py:142
  934.7 21.2 %fusion.227 = f32[1024,128]{1,0:T(8,128)} fusion(f32[512,4,1024]{2,0,1:T(8,128)} %fusion.224, f32[512,4,1024]{2,0,1:T(8,128)} %fusion.225, f32[4,512]{1,0:T(4,128)S(1)} %dynamic-slice_bitcast_fusion.5, pred[512,1024]{1,0:T(8,128)(4,1)} %fusion.226, f32[1024,128]{1,0:T(8,128)} %get-tuple-element.902, ...), kind=kOutput, calls=%fused_computation.71.clone.1 | convolution fusion | flops 560204800 | bytes 36192768 | tf_op jit(solution)/shard_map/while/body/eval_jaxpr/hqk,qhd->kd/dot_general | solution.py:145
  955.9 6.9 fusion.228
  982.8 23.7 %collective-permute-done = bf16[256,512]{1,0:T(8,128)(2,1)S(1)} collective-permute-done((bf16[256,512]{1,0:T(8,128)(2,1)S(1)}, bf16[256,512]{1,0:T(8,128)(2,1)S(1)}, u32[]{:S(2)}, u32[]{:S(2)}) %collective-permute-start) | collective-permute-done | bytes 262176 | tf_op jit(solution)/shard_map/ppermute | solution.py:45
  1006.6 6.5 collective-permute-done.2
  1017.6 5.3 convolution_convert_fusion
  1022.9 8.3 copy.118
  1032.8 6.9 convolution_convert_fusion.2
  1039.6 8.7 copy.119
  1048.4 10.8 fusion.102
  1059.2 15.9 convolution_convert_fusion.1
  1075.1 11.5 pad_maximum_fusion
  1086.6 83.4 %reduce-scatter.13.cloned.1.call-done = bf16[64,2304]{1,0:T(8,128)(2,1)} async-done(((bf16[2048,2304]{1,0:T(8,128)(2,1)}), bf16[64,2304]{1,0:T(8,128)(2,1)}) %reduce-scatter.13.cloned.1.call-update) | async-done | bytes 294928 | tf_op jit(solution)/shard_map/reduce_scatter | solution.py:317
  1170.1 187.1 %reduce-scatter.15.cloned.1.call-done = bf16[64,2048]{1,0:T(8,128)(2,1)} async-done(((bf16[2048,2048]{1,0:T(8,128)(2,1)}), bf16[64,2048]{1,0:T(8,128)(2,1)}) %reduce-scatter.15.cloned.1.call-update) | async-done | bytes 262160 | tf_op jit(solution)/shard_map/reduce_scatter | solution.py:317
  1357.2 161.1 %reduce-scatter.17.cloned.1.call-done = bf16[512,2304]{0,1:T(8,128)(2,1)} async-done(((bf16[2048,2304]{0,1:T(8,128)(2,1)}), bf16[512,2304]{0,1:T(8,128)(2,1)}) %reduce-scatter.17.cloned.1.call-update) | async-done | bytes 2359312 | tf_op jit(solution)/shard_map/reduce_scatter | solution.py:287
  1525.6 9.3 fusion.133
  1534.9 41.5 %psum.7 = f32[2,2048]{1,0:T(2,128)S(1)} all-reduce(f32[2,2048]{1,0:T(2,128)S(1)} %pad_maximum_fusion.13), channel_id=1, replica_groups=mesh['grp'=8,'seq'=4] {'grp','seq'}, use_global_device_ids=true, to_apply=%region_20.21 | all-reduce | flops 4096 | bytes 32768 | tf_op jit(solution)/shard_map/psum | solution.py:351
  1587.1 6.7 copy.120
  1593.8 6.7 copy.121
  1605.4 76.3 %all-gather.27.cloned.1.call-done = bf16[144,512,128]{2,1,0:T(8,128)(2,1)} async-done(((bf16[18,512,128]{2,1,0:T(8,128)(2,1)}), bf16[144,512,128]{2,1,0:T(8,128)(2,1)}) %all-gather.27.cloned.1.call-update) | async-done | bytes 18874384 | tf_op jit(solution)/shard_map/all_gather | solution.py:289
  1681.7 8.9 gather_fusion.5
  1690.6 18.5 %fusion.97 = (f32[21,512,128]{2,1,0:T(8,128)}, f32[21,512,128]{2,1,0:T(8,128)}) fusion(f32[21,512,128]{2,1,0:T(8,128)} %param.24, f32[21,512,128]{2,1,0:T(8,128)} %param.23, f32[21,128,128]{2,1,0:T(8,128)S(1)} %copy-done, f32[21,512,512]{2,1,0:T(8,128)} %param.25, bf16[21,512,128]{2,1,0:T(8,128)(2,1)} %gather_fusion.4, ...), kind=kOutput, calls=%fused_computation.137 | convolution fusion | flops 1772617728 | bytes 50921512 | tf_op jit(solution)/shard_map/zic,zcd->zid/dot_general | solution.py:373
  1709.1 16.1 multiply_subtract_fusion
  (229 shorter events, 157.4 us)
Async XLA Ops:
  7.2 1683.4 %copy-start = (f32[21,128,128]{2,1,0:T(8,128)S(1)}, f32[21,128,128]{2,1,0:T(8,128)}, u32[]{:S(2)}) copy-start(f32[21,128,128]{2,1,0:T(8,128)} %param.26) | copy-start | bytes 4128772
  7.2 117.5 %all-gather.11.cloned.1.call-start = ((), (), s32[]{:S(2)}) async-start(), calls=%async_computation.9 | async-start | bytes 24772608 | tf_op jit(solution)/shard_map/all_gather | solution.py:201
  7.9 174.9 %all-gather.13.cloned.1.call-start = ((), (), s32[]{:S(2)}) async-start(), calls=%async_computation.10 | async-start | bytes 2785280 | tf_op jit(solution)/shard_map/all_gather | solution.py:212
  8.7 174.5 %copy-start.1 = (s32[166]{0:T(256)S(1)}, s32[166]{0:T(256)}, u32[]{:S(2)}) copy-start(s32[166]{0:T(256)} %param.20) | copy-start | bytes 1996
  8.7 175.3 %copy-start.7 = (bf16[256,2048]{1,0:T(8,128)(2,1)S(1)}, bf16[256,2048]{1,0:T(8,128)(2,1)}, u32[]{:S(2)}) copy-start(bf16[256,2048]{1,0:T(8,128)(2,1)} %param.17) | copy-start | bytes 3145732
  134.4 143.5 %all-gather.15.cloned.1.call-start = ((), (), s32[]{:S(2)}) async-start(), calls=%async_computation.11 | async-start | bytes 20054016 | tf_op jit(solution)/shard_map/all_gather | solution.py:213
  182.9 317.0 %all-gather.19.cloned.1.call-start = ((), (), s32[]{:S(2)}) async-start(), calls=%async_computation.13 | async-start | bytes 11796480 | tf_op jit(solution)/shard_map/all_gather | solution.py:220
  194.9 9.3 copy-start.15
  202.7 136.5 %copy-start.22 = (f32[64]{0:T(128)}, f32[64]{0:T(128)S(1)}, u32[]{:S(2)}) copy-start(f32[64]{0:T(128)S(1)} %multiply_power_fusion) | copy-start | bytes 772
  203.3 80.9 %copy-start.19 = (f32[256]{0:T(256)}, f32[256]{0:T(256)S(1)}, u32[]{:S(2)}) copy-start(f32[256]{0:T(256)S(1)} %get-tuple-element.707) | copy-start | bytes 3076
  204.3 80.0 %copy-start.13 = (f32[1,2048]{1,0:T(1,128)}, f32[1,2048]{1,0:T(1,128)S(1)}, u32[]{:S(2)}) copy-start(f32[1,2048]{1,0:T(1,128)S(1)} %get-tuple-element.701) | copy-start | bytes 24580
  291.7 91.5 %all-to-all-start = ((bf16[256,4,512]{0,2,1:T(8,128)(2,1)}), bf16[256,4,512]{0,2,1:T(8,128)(2,1)S(1)}, u32[]{:S(2)}, u32[]{:S(2)}) async-start(bf16[256,4,512]{0,2,1:T(8,128)(2,1)} %bitcast.5), calls=%async_computation | async-start | bytes 2097152 | tf_op jit(solution)/shard_map/all_to_all | solution.py:246
  296.3 258.4 %all-gather.17.cloned.1.call-start = ((), (), s32[]{:S(2)}) async-start(), calls=%async_computation.12 | async-start | bytes 9437184 | tf_op jit(solution)/shard_map/all_gather | solution.py:263
  481.1 129.8 %all-gather.21.cloned.1.call-start = ((), (), s32[]{:S(2)}) async-start(), calls=%async_computation.15 | async-start | bytes 9437184 | tf_op jit(solution)/shard_map/all_gather | solution.py:221
  481.7 237.8 %reduce-scatter.9.cloned.1.call-start = ((), (), s32[]{:S(2)}) async-start(), calls=%async_computation.16 | async-start | bytes 9437184 | tf_op jit(solution)/shard_map/reduce_scatter | solution.py:278
  627.6 1.7 copy-start.26
  648.1 146.6 %reduce-scatter.7.cloned.1.call-start = ((), (), s32[]{:S(2)}) async-start(), calls=%async_computation.14 | async-start | bytes 9437184 | tf_op jit(solution)/shard_map/reduce_scatter | solution.py:290
  798.9 6.5 copy-start.3
  806.5 30.4 %all-to-all-start.2 = ((bf16[256,4,512]{2,0,1:T(8,128)(2,1)}), bf16[256,4,512]{2,0,1:T(8,128)(2,1)}, u32[]{:S(2)}, u32[]{:S(2)}) async-start(bf16[256,4,512]{2,0,1:T(8,128)(2,1)} %bitcast.324), calls=%async_computation.4 | async-start | bytes 2097152 | tf_op jit(solution)/shard_map/all_to_all | solution.py:308
  811.1 205.2 %reduce-scatter.11.cloned.1.call-start = ((), (), s32[]{:S(2)}) async-start(), calls=%async_computation.17 | async-start | bytes 1310720 | tf_op jit(solution)/shard_map/reduce_scatter | solution.py:337
  839.6 127.5 %copy-start.23 = (f32[64]{0:T(128)S(1)}, f32[64]{0:T(128)}, u32[]{:S(2)}) copy-start(f32[64]{0:T(128)} %copy-done.22) | copy-start | bytes 772
  839.6 6.2 copy-start.6
  901.1 6.1 copy-start.6
  962.8 10.7 copy-start.9
  971.5 198.5 %reduce-scatter.13.cloned.1.call-start = ((), (), s32[]{:S(2)}) async-start(), calls=%async_computation.18 | async-start | bytes 9732096 | tf_op jit(solution)/shard_map/reduce_scatter | solution.py:317
  976.7 40.9 %copy-start.8 = (bf16[256,2048]{1,0:T(8,128)(2,1)S(1)}, bf16[256,2048]{1,0:T(8,128)(2,1)}, u32[]{:S(2)}) copy-start(bf16[256,2048]{1,0:T(8,128)(2,1)} %param.17) | copy-start | bytes 3145732
  976.7 40.9 %copy-start.14 = (f32[1,2048]{1,0:T(1,128)S(1)}, f32[1,2048]{1,0:T(1,128)}, u32[]{:S(2)}) copy-start(f32[1,2048]{1,0:T(1,128)} %copy-done.13) | copy-start | bytes 24580
  976.7 40.9 %copy-start.20 = (f32[256]{0:T(256)S(1)}, f32[256]{0:T(256)}, u32[]{:S(2)}) copy-start(f32[256]{0:T(256)} %copy-done.19) | copy-start | bytes 3076
  978.4 28.2 %collective-permute-start = (bf16[256,512]{1,0:T(8,128)(2,1)S(1)}, bf16[256,512]{1,0:T(8,128)(2,1)S(1)}, u32[]{:S(2)}, u32[]{:S(2)}) collective-permute-start(bf16[256,512]{1,0:T(8,128)(2,1)S(1)} %get-tuple-element.693), channel_id=1, source_target_pairs={{0,1},{1,0},{2,3},{3,2},{4,5},{5,4},{6,7},{7,6},{8,9},{9,8},{10,11... | collective-permute-start | bytes 786440 | tf_op jit(solution)/shard_map/ppermute | solution.py:45
  978.4 28.1 %collective-permute-start.1 = (bf16[256,512]{1,0:T(8,128)(2,1)S(1)}, bf16[256,512]{1,0:T(8,128)(2,1)S(1)}, u32[]{:S(2)}, u32[]{:S(2)}) collective-permute-start(bf16[256,512]{1,0:T(8,128)(2,1)S(1)} %get-tuple-element.692), channel_id=1, source_target_pairs={{0,2},{1,3},{2,0},{3,1},{4,6},{5,7},{6,4},{7,5},{8,10},{9,11},{10,... | collective-permute-start | bytes 786440 | tf_op jit(solution)/shard_map/ppermute | solution.py:45
  980.4 32.7 %collective-permute-start.2 = (bf16[256,512]{1,0:T(8,128)(2,1)S(1)}, bf16[256,512]{1,0:T(8,128)(2,1)S(1)}, u32[]{:S(2)}, u32[]{:S(2)}) collective-permute-start(bf16[256,512]{1,0:T(8,128)(2,1)S(1)} %get-tuple-element.691), channel_id=1, source_target_pairs={{0,3},{1,2},{2,1},{3,0},{4,7},{5,6},{6,5},{7,4},{8,11},{9,10},{10,... | collective-permute-start | bytes 786440 | tf_op jit(solution)/shard_map/ppermute | solution.py:45
  1016.3 6.6 copy-start.10
  1017.5 5.4 copy-start.12
  1031.2 1.6 copy-start.4
  1031.2 326.0 %reduce-scatter.15.cloned.1.call-start = ((), (), s32[]{:S(2)}) async-start(), calls=%async_computation.20 | async-start | bytes 8650752 | tf_op jit(solution)/shard_map/reduce_scatter | solution.py:317
  1048.3 470.0 %reduce-scatter.17.cloned.1.call-start = ((), (), s32[]{:S(2)}) async-start(), calls=%async_computation.22 | async-start | bytes 11796480 | tf_op jit(solution)/shard_map/reduce_scatter | solution.py:287
  1048.4 10.8 copy-start.27
  1048.4 10.8 copy-start.28
  1086.6 436.1 %copy-start.2 = (s32[166]{0:T(256)S(1)}, s32[166]{0:T(256)}, u32[]{:S(2)}) copy-start(s32[166]{0:T(256)} %param.20) | copy-start | bytes 1996
  1086.6 495.8 %all-gather.23.cloned.1.call-start = ((), (), s32[]{:S(2)}) async-start(), calls=%async_computation.19 | async-start | bytes 2654208 | tf_op jit(solution)/shard_map/all_gather | solution.py:318
  1170.0 412.4 %all-gather.25.cloned.1.call-start = ((), (), s32[]{:S(2)}) async-start(), calls=%async_computation.21 | async-start | bytes 2359296 | tf_op jit(solution)/shard_map/all_gather | solution.py:318
  1357.2 324.5 %all-gather.27.cloned.1.call-start = ((), (), s32[]{:S(2)}) async-start(), calls=%async_computation.23 | async-start | bytes 21233664 | tf_op jit(solution)/shard_map/all_gather | solution.py:289
  1525.6 9.3 copy-start.18
  1525.6 51.6 %copy-start.16 = (f32[2,2048]{1,0:T(2,128)S(1)}, f32[2,2048]{1,0:T(2,128)}, u32[]{:S(2)}) copy-start(f32[2,2048]{1,0:T(2,128)} %param.27) | copy-start | bytes 49156
  1525.6 51.6 %copy-start.21 = (f32[2,2048]{1,0:T(2,128)S(1)}, f32[2,2048]{1,0:T(2,128)}, u32[]{:S(2)}) copy-start(f32[2,2048]{1,0:T(2,128)} %param.28) | copy-start | bytes 49156
  1576.4 10.6 copy-start.17
  1600.4 90.2 %copy-start.24 = (pred[21]{0:T(512)(128)(4,1)S(1)}, pred[21]{0:T(512)(128)(4,1)}, u32[]{:S(2)}) copy-start(pred[21]{0:T(512)(128)(4,1)} %get-tuple-element.671) | copy-start | bytes 67
  1600.4 90.2 %copy-start.25 = (pred[21]{0:T(512)(128)(4,1)S(1)}, pred[21]{0:T(512)(128)(4,1)}, u32[]{:S(2)}) copy-start(pred[21]{0:T(512)(128)(4,1)} %broadcast_compare_fusion) | copy-start | bytes 67
  (2 other events, 2.7 us)
Sparse Core Ops, SparseCore 0:
  9.9 114.7 all-gather.10
  134.5 48.3 all-gather.12
  184.8 93.1 all-gather.14
  279.9 219.8 all-gather.18
  502.1 52.5 all-gather.16
  556.5 54.3 all-gather.20
  648.2 71.2 reduce-scatter.8
  723.4 71.2 reduce-scatter.6
  971.7 40.6 reduce-scatter.10
  1031.3 138.6 reduce-scatter.12
  1172.3 184.8 reduce-scatter.14
  1359.4 158.9 reduce-scatter.16
  1520.3 30.3 all-gather.22
  1552.4 28.3 all-gather.24
  1583.1 98.5 all-gather.26
